TPU v7x, 512 devices: a whole 4x8x8 slice. The times are simulated.
512 devices in a mesh: ctx: 64 (over x, z, core), head: 8 (over y).
Axes of the slice: x: 4, y: 8, z: 8, core: 2. Of those that a mesh axis runs over, the one named last changes fastest.
Arguments:
- dec_states: bfloat16 [16384, 4096], P('ctx', 'head'), may hold values from -512 to 512
- norm_gain: float32 [4096], replicated, may hold values from 0.1 to 1.9
- w_query: bfloat16 [4096, 4096], P('ctx', 'head'), may hold values from -0.09375 to 0.09375
- enc_keys: bfloat16 [131072, 4096], P('ctx', 'head'), may hold values from -128 to 128
- enc_values: bfloat16 [131072, 4096], P('ctx', 'head'), may hold values from -24 to 24
- w_out: bfloat16 [4096, 4096], P('ctx', 'head'), may hold values from -0.09375 to 0.09375
- tgt_lengths: int32 [32], replicated, may hold values from 1 to 512, 8192 in all
- src_lengths: int32 [32], replicated, may hold values from 2049 to 4096, as said below
Outputs:
- attn_output: bfloat16 [16384, 4096], P('ctx', 'head')
Inputs may be any that keep to these rules, and one draw needn't show every extreme that they name: `tgt_lengths`: the lengths sum to 8192, and the longest equals 512. `src_lengths`: every example has more than 2048 encoder rows, and some example has all 4096.
All inputs are finite; a program needn't handle non-finite values.
Results may differ from a plain program's by a relative error of at most 0.009.
Values may be sent and summed in bfloat16 or wider, within the bound.
No kernel may reach another device: no remote copies, remote signals or barrier semaphores. Data moves between devices by JAX's collectives and lax.ppermute only.
A program may use at most 64 MiB of HBM per device.

v0:
```python
import jax
import jax.numpy as jnp
from jax import lax
from jax.sharding import PartitionSpec as P

DK = 64


def partner(value, axis, distance):
    mask = 2**distance
    pairs = [(source, source ^ mask) for source in range(lax.axis_size(axis))]
    return lax.ppermute(value, axis, pairs)


def attend(queries, keys, values, key_valid):
    row_count = queries.shape[0]
    head_count = queries.shape[1] // DK
    query_heads = jnp.moveaxis(queries.reshape(row_count, head_count, DK), 1, 0)
    key_heads = jnp.moveaxis(keys.reshape(-1, head_count, DK), 1, 0)
    value_heads = jnp.moveaxis(values.reshape(-1, head_count, DK), 1, 0)

    def one_head(head_items):
        query_head, key_head, value_head = head_items
        scores = jnp.dot(query_head, key_head.T, preferred_element_type=jnp.float32)
        scores = jnp.where(key_valid[None, :], scores, -jnp.inf)
        top_score = jnp.max(scores, axis=1)
        weights = jnp.exp(scores - top_score[:, None]).astype(jnp.bfloat16)
        totals = jnp.sum(weights.astype(jnp.float32), axis=1)
        weighted = jnp.dot(weights, value_head, preferred_element_type=jnp.float32)
        return (top_score, totals, weighted)

    top_score, totals, weighted = lax.map(one_head, (query_heads, key_heads, value_heads))
    return (top_score.T, totals.T, jnp.moveaxis(weighted, 0, 1).reshape(row_count, head_count * DK))


def combine_halves(first, second):
    top_one, totals_one, weighted_one = first
    top_two, totals_two, weighted_two = second
    row_count = weighted_one.shape[0]
    head_count = top_one.shape[1]
    largest = jnp.maximum(top_one, top_two)
    scale_one = jnp.exp(top_one - largest)
    scale_two = jnp.exp(top_two - largest)
    numer = (
        weighted_one.reshape(row_count, head_count, DK) * scale_one[:, :, None]
        + weighted_two.reshape(row_count, head_count, DK) * scale_two[:, :, None]
    )
    denom = totals_one * scale_one + totals_two * scale_two
    return (numer / denom[:, :, None]).reshape(row_count, head_count * DK)


def local(dec_states, norm_gain, w_query, enc_keys, enc_values, w_out, tgt_lengths, src_lengths):
    position = lax.axis_index("ctx")
    half_index = position % 2
    example = position // 2
    slot_ids = jnp.arange(tgt_lengths.shape[0], dtype=jnp.int32)
    tgt_len = jnp.sum(jnp.where(slot_ids == example, tgt_lengths, 0))
    src_len = jnp.sum(jnp.where(slot_ids == example, src_lengths, 0))
    enc_count = enc_keys.shape[0]
    full_states = lax.all_gather(dec_states, "head", axis=1, tiled=True)
    row_count = full_states.shape[0]
    states = full_states.astype(jnp.float32)
    normed = (
        states * lax.rsqrt(jnp.mean(states * states, axis=-1, keepdims=True) + 1e-06) * norm_gain
    ).astype(jnp.bfloat16)
    columns = normed
    queries = jnp.dot(
        columns,
        lax.all_gather(w_query, "ctx", axis=0, tiled=True),
        preferred_element_type=jnp.float32,
    ).astype(jnp.bfloat16)
    offsets = jnp.arange(enc_count, dtype=jnp.int32)
    own_valid = half_index * enc_count + offsets < src_len
    far_valid = (1 - half_index) * enc_count + offsets < src_len
    far_keys, far_values = partner((enc_keys, enc_values), "ctx", 0)
    nearby = attend(queries, enc_keys, enc_values, own_valid)
    distant = attend(queries, far_keys, far_values, far_valid)
    attended = combine_halves(nearby, distant)
    live_rows = half_index * row_count + jnp.arange(row_count, dtype=jnp.int32) < tgt_len
    attended = jnp.where(live_rows[:, None], attended, 0.0).astype(jnp.bfloat16)
    all_heads = lax.all_gather(attended, "head", axis=1, tiled=True)
    columns = all_heads
    projected = jnp.dot(
        columns,
        lax.all_gather(w_out, "ctx", axis=0, tiled=True),
        preferred_element_type=jnp.float32,
    )
    return projected.astype(jnp.bfloat16)


def solution(mesh):
    placed = (
        P("ctx", "head"),
        P(),
        P("ctx", "head"),
        P("ctx", "head"),
        P("ctx", "head"),
        P("ctx", "head"),
        P(),
        P(),
    )
    return jax.shard_map(
        local, mesh=mesh, in_specs=placed, out_specs=P("ctx", "head"), check_vma=False
    )
```

profile of v0, /device:TPU:2, one launch (start us, length us, event | category | flops | bytes accessed | tf_op | source)
XLA Modules:
  0.0 284.5 jit_solution(14177036345322470178)
XLA Ops:
  8.1 2.9 %copy.11 = bf16[2048,512]{0,1:T(8,128)(2,1)S(1)} copy(bf16[2048,512]{1,0:T(8,128)(2,1)} %param.15) | data formatting | bytes 4194304 | tf_op args[3]
  11.0 1.9 collective-permute-start
  12.9 4.0 %copy.12 = bf16[2048,512]{0,1:T(8,128)(2,1)} copy(bf16[2048,512]{1,0:T(8,128)(2,1)} %param.16) | data formatting | bytes 4194304 | tf_op args[4]
  16.9 2.5 collective-permute-start.1
  21.5 36.2 %all-gather.5.cloned.1.call-done = bf16[256,4096]{1,0:T(8,128)(2,1)} async-done(((bf16[256,512]{1,0:T(8,128)(2,1)}), bf16[256,4096]{1,0:T(8,128)(2,1)}) %all-gather.5.cloned.1.call-update) | async-done | bytes 2097168 | tf_op jit(solution)/shard_map/all_gather | solution.py:60
  57.7 2.1 fusion.22
  59.8 84.6 %all-gather.7.cloned.1.call-done = bf16[4096,512]{1,0:T(8,128)(2,1)} async-done(((bf16[64,512]{1,0:T(8,128)(2,1)}), bf16[4096,512]{1,0:T(8,128)(2,1)}) %all-gather.7.cloned.1.call-update) | async-done | bytes 4194320 | tf_op jit(solution)/shard_map/all_gather | solution.py:69
  144.4 4.1 %fusion.29 = bf16[256,512]{1,0:T(8,128)(2,1)S(1)} fusion(bf16[4096,512]{1,0:T(8,128)(2,1)} %all-gather.7.cloned.1.call-done, bf16[256,4096]{1,0:T(8,128)(2,1)} %all-gather.5.cloned.1.call-done, f32[4096]{0:T(1024)S(1)} %copy-done.1, f32[256]{0:T(256)S(1)} %add_rsqrt_fusion), kind=kOutput, calls=%fused_computation.38 | convolution fusion | flops 1078067200 | bytes 6571008 | tf_op jit(solution)/shard_map/dot_general | solution.py:67
  149.0 32.8 %while.31 = (s32[]{:T(128)}, f32[8,256]{1,0:T(8,128)S(1)}, f32[8,256]{1,0:T(8,128)S(1)}, f32[8,256,64]{1,2,0:T(8,128)S(1)}, bf16[8,256,64]{2,1,0:T(8,128)(2,1)S(...) while((s32[]{:T(128)}, f32[8,256]{1,0:T(8,128)S(1)}, ...), condition=%wide.region_10.11_spmd.clone, body=%wide.region_7.10_spmd.clone.sunk | while | flops 138415616 | bytes 6961277 | solution.py:32
  151.1 1.5 fusion.58
  155.2 1.5 fusion.58
  157.8 1.5 fusion.57
  159.3 1.5 fusion.58
  163.4 1.5 fusion.58
  167.5 1.5 fusion.58
  170.1 1.4 fusion.57
  171.6 1.5 fusion.58
  175.7 1.5 fusion.58
  178.3 1.4 fusion.57
  179.8 1.5 fusion.58
  182.6 25.2 %while.30 = (s32[]{:T(128)}, f32[8,256]{1,0:T(8,128)S(1)}, f32[8,256]{1,0:T(8,128)S(1)}, f32[8,256,64]{1,2,0:T(8,128)S(1)}, bf16[8,256,64]{2,1,0:T(8,128)(2,1)S(...) while((s32[]{:T(128)}, f32[8,256]{1,0:T(8,128)S(1)}, ...), condition=%wide.region_6.7_spmd.clone, body=%wide.region_3.6_spmd.clone.sunk | while | flops 138415616 | bytes 6961277 | solution.py:32
  183.8 1.5 fusion.55
  186.9 1.5 fusion.55
  190.1 1.5 fusion.55
  193.2 1.5 fusion.55
  196.4 1.5 fusion.55
  199.5 1.5 fusion.55
  202.7 1.5 fusion.55
  205.8 1.5 fusion.55
  209.8 19.9 %all-gather.11.cloned.1.call-done = bf16[4096,512]{1,0:T(8,128)(2,1)} async-done(((bf16[64,512]{1,0:T(8,128)(2,1)}), bf16[4096,512]{1,0:T(8,128)(2,1)}) %all-gather.11.cloned.1.call-update) | async-done | bytes 4194320 | tf_op jit(solution)/shard_map/all_gather | solution.py:85
  229.7 43.5 %all-gather.9.cloned.1.call-done = bf16[256,4096]{0,1:T(8,128)(2,1)} async-done(((bf16[256,512]{0,1:T(8,128)(2,1)}), bf16[256,4096]{0,1:T(8,128)(2,1)}) %all-gather.9.cloned.1.call-update) | async-done | bytes 2097168 | tf_op jit(solution)/shard_map/all_gather | solution.py:81
  273.1 4.8 %convolution_convert_fusion = bf16[256,512]{1,0:T(8,128)(2,1)} fusion(bf16[256,4096]{0,1:T(8,128)(2,1)} %all-gather.9.cloned.1.call-done, bf16[4096,512]{1,0:T(8,128)(2,1)} %all-gather.11.cloned.1.call-done), kind=kOutput, calls=%fused_computation.39 | convolution fusion | flops 1073872896 | bytes 6553600 | tf_op jit(solution)/shard_map/dot_general | solution.py:83
  (110 shorter events, 36.2 us)
Async XLA Ops:
  6.5 51.2 %all-gather.5.cloned.1.call-start = ((), (), s32[]{:S(2)}) async-start(), calls=%async_computation | async-start | bytes 2359296 | tf_op jit(solution)/shard_map/all_gather | solution.py:60
  7.3 137.1 %all-gather.7.cloned.1.call-start = ((), (), s32[]{:S(2)}) async-start(), calls=%async_computation.1 | async-start | bytes 4259840 | tf_op jit(solution)/shard_map/all_gather | solution.py:69
  8.0 221.6 %all-gather.11.cloned.1.call-start = ((), (), s32[]{:S(2)}) async-start(), calls=%async_computation.3 | async-start | bytes 4259840 | tf_op jit(solution)/shard_map/all_gather | solution.py:85
  11.0 8.6 %copy-start.2 = (s32[32]{0:T(128)S(1)}, s32[32]{0:T(128)}, u32[]{:S(2)}) copy-start(s32[32]{0:T(128)} %param.18) | copy-start | bytes 388
  11.0 9.8 %copy-start.3 = (s32[32]{0:T(128)S(1)}, s32[32]{0:T(128)}, u32[]{:S(2)}) copy-start(s32[32]{0:T(128)} %param.19) | copy-start | bytes 388
  11.0 137.9 %collective-permute-start = (bf16[2048,512]{0,1:T(8,128)(2,1)S(1)}, bf16[2048,512]{0,1:T(8,128)(2,1)}, u32[]{:S(2)}, u32[]{:S(2)}) collective-permute-start(bf16[2048,512]{0,1:T(8,128)(2,1)S(1)} %copy.11), channel_id=1, source_target_pairs={{0,8},{8,0},{16,24},{24,16},{32,40},{40,32},{48,56},{56,48},{64,72... | collective-permute-start | bytes 6291464 | tf_op jit(solution)/shard_map/ppermute | solution.py:12
  16.9 127.4 %copy-start.1 = (f32[4096]{0:T(1024)S(1)}, f32[4096]{0:T(1024)}, u32[]{:S(2)}) copy-start(f32[4096]{0:T(1024)} %param.13) | copy-start | bytes 49156
  16.9 132.0 %collective-permute-start.1 = (bf16[2048,512]{0,1:T(8,128)(2,1)}, bf16[2048,512]{0,1:T(8,128)(2,1)}, u32[]{:S(2)}, u32[]{:S(2)}) collective-permute-start(bf16[2048,512]{0,1:T(8,128)(2,1)} %copy.12), channel_id=1, source_target_pairs={{0,8},{8,0},{16,24},{24,16},{32,40},{40,32},{48,56},{56,48},{64,72... | collective-permute-start | bytes 6291464 | tf_op jit(solution)/shard_map/ppermute | solution.py:12
  19.5 253.7 %all-gather.9.cloned.1.call-start = ((), (), s32[]{:S(2)}) async-start(), calls=%async_computation.2 | async-start | bytes 2359296 | tf_op jit(solution)/shard_map/all_gather | solution.py:81
  181.8 0.8 copy-start
Sparse Core Ops, SparseCore 0:
  9.4 48.2 all-gather.4
  61.1 83.2 all-gather.6
  147.7 81.8 all-gather.10
  231.6 41.5 all-gather.8
where the time goes:
time: 286 us; the launch traced here: 284 us
  waiting for transfers between devices  186 us (65%)
  matrix products  48 us (17%)
  other arithmetic  22.9 us (8%)
  between operations  13.3 us (5%)
  local copies, waits for them, and re-layouts  9.49 us (3%)
  starting transfers between devices  4.57 us (2%)
    all_gather x1, waiting for transfers between devices, local(): lax.all_gather(w_query, 'ctx', axis=0, tiled=True)  84.6 us
    all_gather x1, waiting for transfers between devices, local(): all_heads = lax.all_gather(attended, 'head', axis=1, tiled=True)  43.5 us
    all_gather x1, waiting for transfers between devices, local(): full_states = lax.all_gather(dec_states, 'head', axis=1, tiled=True)  36.2 us
    dot_general x16, matrix products, one_head(): weighted = jnp.dot(weights, value_head, preferred_element_type=jnp.float32)  23.5 us
    all_gather x1, waiting for transfers between devices, local(): lax.all_gather(w_out, 'ctx', axis=0, tiled=True)  19.9 us
    dot_general x16, matrix products, one_head(): scores = jnp.dot(query_head, key_head.T, preferred_element_type=jnp.float32)  15.6 us
    unnamed x11, local copies, waits for them, and re-layouts  7.97 us
    reduce_sum x16, other arithmetic, one_head(): totals = jnp.sum(weights.astype(jnp.float32), axis=1)  6.97 us
  transfers between devices with their start and end apart: 6, of which 4 were waited for; matrix products, arithmetic and copies ran while one was open for 26% of the time, Pallas kernels for 0%

commit v1 on v0

--- a/solution.py
+++ b/solution.py
@@ -2,6 +2,7 @@
 import jax.numpy as jnp
 from jax import lax
 from jax.sharding import PartitionSpec as P
+from jax.lax import axis_index, axis_size, ppermute
 
 DK = 64
 
@@ -78,7 +79,21 @@
     attended = combine_halves(nearby, distant)
     live_rows = half_index * row_count + jnp.arange(row_count, dtype=jnp.int32) < tgt_len
     attended = jnp.where(live_rows[:, None], attended, 0.0).astype(jnp.bfloat16)
-    all_heads = lax.all_gather(attended, "head", axis=1, tiled=True)
+
+    def switch_sources_all(frame_in):
+        axis_total = axis_size("head")
+        ledger = list(map(lambda src_i: (src_i, (src_i + 1) % axis_total), range(axis_total)))
+        vals = list(map(lambda src_i: (src_i, (src_i - 1) % axis_total), range(axis_total)))
+        current_arr, shaped = ([frame_in], [frame_in])
+        for _ in range(axis_total // 2):
+            current_arr.append(ppermute(current_arr[-1], "head", ledger))
+        for _ in range((axis_total - 1) // 2):
+            shaped.append(ppermute(shaped[-1], "head", vals))
+        x_new = jnp.concatenate([*current_arr[::-1], *shaped[1:]], 1)
+        k_now = jnp.roll(x_new, (axis_index("head") - axis_total // 2) * frame_in.shape[1], 1)
+        return k_now
+
+    all_heads = switch_sources_all(attended)
     columns = all_heads
     projected = jnp.dot(
         columns,

time: 286 us -> 277 us (0.969)
  the two profiles are of different devices: /device:TPU:2 before, /device:TPU:32 now
where the time goes in v1:
time: 277 us; the launch traced here: 275 us
  waiting for transfers between devices  141 us (51%)
  matrix products  48 us (17%)
  starting transfers between devices  28 us (10%)
  other arithmetic  23.5 us (8%)
  local copies, waits for them, and re-layouts  21.1 us (8%)
  between operations  13.4 us (5%)
    all_gather x1, waiting for transfers between devices, local(): lax.all_gather(w_query, 'ctx', axis=0, tiled=True)  87.7 us
    all_gather x1, waiting for transfers between devices, local(): full_states = lax.all_gather(dec_states, 'head', axis=1, tiled=True)  33.7 us
    dot_general x16, matrix products, one_head(): weighted = jnp.dot(weights, value_head, preferred_element_type=jnp.float32)  23.5 us
    unnamed x26, local copies, waits for them, and re-layouts  18.8 us
    ppermute x4, waiting for transfers between devices, switch_sources_all(): current_arr.append(ppermute(current_arr[-1], 'head', ledger))  17.9 us
    dot_general x16, matrix products, one_head(): scores = jnp.dot(query_head, key_head.T, preferred_element_type=jnp.float32)  15.6 us
    ppermute x3, starting transfers between devices, switch_sources_all(): shaped.append(ppermute(shaped[-1], 'head', vals))  15.4 us
    ppermute x4, starting transfers between devices, switch_sources_all(): current_arr.append(ppermute(current_arr[-1], 'head', ledger))  8.22 us
  transfers between devices with their start and end apart: 12, of which 6 were waited for; matrix products, arithmetic and copies ran while one was open for 32% of the time, Pallas kernels for 0%

profile of v1, /device:TPU:32, one launch (start us, length us, event | category | flops | bytes accessed | tf_op | source)
XLA Modules:
  0.0 275.4 jit_solution(17765567889346647853)
XLA Ops:
  8.1 2.9 %copy.11 = bf16[2048,512]{0,1:T(8,128)(2,1)S(1)} copy(bf16[2048,512]{1,0:T(8,128)(2,1)} %param.15) | data formatting | bytes 4194304 | tf_op args[3]
  11.0 1.9 collective-permute-start
  13.0 4.0 %copy.12 = bf16[2048,512]{0,1:T(8,128)(2,1)} copy(bf16[2048,512]{1,0:T(8,128)(2,1)} %param.16) | data formatting | bytes 4194304 | tf_op args[4]
  16.9 2.4 collective-permute-start.1
  21.5 33.7 %all-gather.4.cloned.1.call-done = bf16[256,4096]{1,0:T(8,128)(2,1)} async-done(((bf16[256,512]{1,0:T(8,128)(2,1)}), bf16[256,4096]{1,0:T(8,128)(2,1)}) %all-gather.4.cloned.1.call-update) | async-done | bytes 2097168 | tf_op jit(solution)/shard_map/all_gather | solution.py:61
  55.2 2.1 fusion.22
  57.3 87.7 %all-gather.6.cloned.1.call-done = bf16[4096,512]{1,0:T(8,128)(2,1)} async-done(((bf16[64,512]{1,0:T(8,128)(2,1)}), bf16[4096,512]{1,0:T(8,128)(2,1)}) %all-gather.6.cloned.1.call-update) | async-done | bytes 4194320 | tf_op jit(solution)/shard_map/all_gather | solution.py:70
  145.0 4.1 %fusion.34 = bf16[256,512]{1,0:T(8,128)(2,1)S(1)} fusion(bf16[4096,512]{1,0:T(8,128)(2,1)} %all-gather.6.cloned.1.call-done, bf16[256,4096]{1,0:T(8,128)(2,1)} %all-gather.4.cloned.1.call-done, f32[4096]{0:T(1024)S(1)} %copy-done.1, f32[256]{0:T(256)S(1)} %add_rsqrt_fusion), kind=kOutput, calls=%fused_computation.41 | convolution fusion | flops 1078067200 | bytes 6571008 | tf_op jit(solution)/shard_map/dot_general | solution.py:68
  149.7 33.3 %while.31 = (s32[]{:T(128)}, f32[8,256]{1,0:T(8,128)S(1)}, f32[8,256]{1,0:T(8,128)S(1)}, f32[8,256,64]{1,2,0:T(8,128)S(1)}, bf16[8,256,64]{2,1,0:T(8,128)(2,1)S(...) while((s32[]{:T(128)}, f32[8,256]{1,0:T(8,128)S(1)}, ...), condition=%wide.region_10.11_spmd.clone, body=%wide.region_7.10_spmd.clone.sunk | while | flops 138415616 | bytes 6961277 | solution.py:33
  151.8 1.5 fusion.63
  156.0 1.5 fusion.63
  160.2 1.5 fusion.63
  172.7 1.5 fusion.63
  181.0 1.5 fusion.63
  183.9 25.7 %while.30 = (s32[]{:T(128)}, f32[8,256]{1,0:T(8,128)S(1)}, f32[8,256]{1,0:T(8,128)S(1)}, f32[8,256,64]{1,2,0:T(8,128)S(1)}, bf16[8,256,64]{2,1,0:T(8,128)(2,1)S(...) while((s32[]{:T(128)}, f32[8,256]{1,0:T(8,128)S(1)}, ...), condition=%wide.region_6.7_spmd.clone, body=%wide.region_3.6_spmd.clone.sunk | while | flops 138415616 | bytes 6961277 | solution.py:33
  185.1 1.5 fusion.60
  191.5 1.5 fusion.60
  194.7 1.5 fusion.60
  197.9 1.5 fusion.60
  201.2 1.5 fusion.60
  210.8 2.5 collective-permute-start.2
  213.3 9.1 %collective-permute-done.2 = bf16[256,512]{0,1:T(8,128)(2,1)S(1)} collective-permute-done((bf16[256,512]{0,1:T(8,128)(2,1)S(1)}, bf16[256,512]{0,1:T(8,128)(2,1)S(1)}, u32[]{:S(2)}, u32[]{:S(2)}) %collective-permute-start.2) | collective-permute-done | bytes 262176 | tf_op jit(solution)/shard_map/ppermute | solution.py:89
  222.4 1.9 collective-permute-start.3
  224.3 5.1 %collective-permute-start.6 = (bf16[256,512]{0,1:T(8,128)(2,1)S(1)}, bf16[256,512]{0,1:T(8,128)(2,1)S(1)}, u32[]{:S(2)}, u32[]{:S(2)}) collective-permute-start(bf16[256,512]{0,1:T(8,128)(2,1)S(1)} %fusion.37), channel_id=1, source_target_pairs={{0,7},{1,0},{2,1},{3,2},{4,3},{5,4},{6,5},{7,6},{8,15},{9,8},{10,9... | collective-permute-start | bytes 786440 | tf_op jit(solution)/shard_map/ppermute | solution.py:91
  229.5 3.7 %collective-permute-done.3 = bf16[256,512]{0,1:T(8,128)(2,1)S(1)} collective-permute-done((bf16[256,512]{0,1:T(8,128)(2,1)S(1)}, bf16[256,512]{0,1:T(8,128)(2,1)S(1)}, u32[]{:S(2)}, u32[]{:S(2)}) %collective-permute-start.3) | collective-permute-done | bytes 262176 | tf_op jit(solution)/shard_map/ppermute | solution.py:89
  233.2 1.9 collective-permute-start.4
  235.1 5.1 %collective-permute-start.7 = (bf16[256,512]{0,1:T(8,128)(2,1)S(1)}, bf16[256,512]{0,1:T(8,128)(2,1)S(1)}, u32[]{:S(2)}, u32[]{:S(2)}) collective-permute-start(bf16[256,512]{0,1:T(8,128)(2,1)S(1)} %collective-permute-done.6), channel_id=1, source_target_pairs={{0,7},{1,0},{2,1},{3,2},{4,3},{5,4},{6,5},{7,6},{8,15},{9,8},{10,9... | collective-permute-start | bytes 786440 | tf_op jit(solution)/shard_map/ppermute | solution.py:91
  240.2 2.8 %collective-permute-done.4 = bf16[256,512]{0,1:T(8,128)(2,1)S(1)} collective-permute-done((bf16[256,512]{0,1:T(8,128)(2,1)S(1)}, bf16[256,512]{0,1:T(8,128)(2,1)S(1)}, u32[]{:S(2)}, u32[]{:S(2)}) %collective-permute-start.4) | collective-permute-done | bytes 262176 | tf_op jit(solution)/shard_map/ppermute | solution.py:89
  243.0 1.9 collective-permute-start.5
  244.9 5.1 %collective-permute-start.8 = (bf16[256,512]{0,1:T(8,128)(2,1)S(1)}, bf16[256,512]{0,1:T(8,128)(2,1)S(1)}, u32[]{:S(2)}, u32[]{:S(2)}) collective-permute-start(bf16[256,512]{0,1:T(8,128)(2,1)S(1)} %collective-permute-done.7), channel_id=1, source_target_pairs={{0,7},{1,0},{2,1},{3,2},{4,3},{5,4},{6,5},{7,6},{8,15},{9,8},{10,9... | collective-permute-start | bytes 786440 | tf_op jit(solution)/shard_map/ppermute | solution.py:91
  250.1 2.4 collective-permute-done.5
  264.1 4.8 %fusion.31 = bf16[256,512]{1,0:T(8,128)(2,1)} fusion(bf16[4096,512]{1,0:T(8,128)(2,1)} %all-gather.8.cloned.1.call-done, bf16[256,8192]{0,1:T(8,128)(2,1)} %constant_dynamic-update-slice_fusion, s32[]{:T(128)S(6)} %select_n.47), kind=kOutput, calls=%fused_computation.40 | convolution fusion | flops 1073872896 | bytes 6553604 | tf_op jit(solution)/shard_map/dot_general | solution.py:98
  (137 shorter events, 61.6 us)
Async XLA Ops:
  6.5 48.7 %all-gather.4.cloned.1.call-start = ((), (), s32[]{:S(2)}) async-start(), calls=%async_computation | async-start | bytes 2359296 | tf_op jit(solution)/shard_map/all_gather | solution.py:61
  7.3 137.8 %all-gather.6.cloned.1.call-start = ((), (), s32[]{:S(2)}) async-start(), calls=%async_computation.1 | async-start | bytes 4259840 | tf_op jit(solution)/shard_map/all_gather | solution.py:70
  8.0 11.4 %copy-start.2 = (s32[32]{0:T(128)S(1)}, s32[32]{0:T(128)}, u32[]{:S(2)}) copy-start(s32[32]{0:T(128)} %param.18) | copy-start | bytes 388
  8.0 12.8 %copy-start.3 = (s32[32]{0:T(128)S(1)}, s32[32]{0:T(128)}, u32[]{:S(2)}) copy-start(s32[32]{0:T(128)} %param.19) | copy-start | bytes 388
  8.0 256.1 %all-gather.8.cloned.1.call-start = ((), (), s32[]{:S(2)}) async-start(), calls=%async_computation.2 | async-start | bytes 4259840 | tf_op jit(solution)/shard_map/all_gather | solution.py:100
  11.0 134.0 %copy-start.1 = (f32[4096]{0:T(1024)S(1)}, f32[4096]{0:T(1024)}, u32[]{:S(2)}) copy-start(f32[4096]{0:T(1024)} %param.13) | copy-start | bytes 49156
  11.0 138.6 %collective-permute-start = (bf16[2048,512]{0,1:T(8,128)(2,1)S(1)}, bf16[2048,512]{0,1:T(8,128)(2,1)}, u32[]{:S(2)}, u32[]{:S(2)}) collective-permute-start(bf16[2048,512]{0,1:T(8,128)(2,1)S(1)} %copy.11), channel_id=1, source_target_pairs={{0,8},{8,0},{16,24},{24,16},{32,40},{40,32},{48,56},{56,48},{64,72... | collective-permute-start | bytes 6291464 | tf_op jit(solution)/shard_map/ppermute | solution.py:13
  16.9 132.7 %collective-permute-start.1 = (bf16[2048,512]{0,1:T(8,128)(2,1)}, bf16[2048,512]{0,1:T(8,128)(2,1)}, u32[]{:S(2)}, u32[]{:S(2)}) collective-permute-start(bf16[2048,512]{0,1:T(8,128)(2,1)} %copy.12), channel_id=1, source_target_pairs={{0,8},{8,0},{16,24},{24,16},{32,40},{40,32},{48,56},{56,48},{64,72... | collective-permute-start | bytes 6291464 | tf_op jit(solution)/shard_map/ppermute | solution.py:13
  183.0 0.8 copy-start
  210.8 11.6 %collective-permute-start.2 = (bf16[256,512]{0,1:T(8,128)(2,1)S(1)}, bf16[256,512]{0,1:T(8,128)(2,1)S(1)}, u32[]{:S(2)}, u32[]{:S(2)}) collective-permute-start(bf16[256,512]{0,1:T(8,128)(2,1)S(1)} %fusion.37), channel_id=1, source_target_pairs={{0,1},{1,2},{2,3},{3,4},{4,5},{5,6},{6,7},{7,0},{8,9},{9,10},{10,1... | collective-permute-start | bytes 786440 | tf_op jit(solution)/shard_map/ppermute | solution.py:89
  222.4 10.8 %collective-permute-start.3 = (bf16[256,512]{0,1:T(8,128)(2,1)S(1)}, bf16[256,512]{0,1:T(8,128)(2,1)S(1)}, u32[]{:S(2)}, u32[]{:S(2)}) collective-permute-start(bf16[256,512]{0,1:T(8,128)(2,1)S(1)} %collective-permute-done.2), channel_id=1, source_target_pairs={{0,1},{1,2},{2,3},{3,4},{4,5},{5,6},{6,7},{7,0},{8,9},{9,10},{10,1... | collective-permute-start | bytes 786440 | tf_op jit(solution)/shard_map/ppermute | solution.py:89
  224.3 10.8 %collective-permute-start.6 = (bf16[256,512]{0,1:T(8,128)(2,1)S(1)}, bf16[256,512]{0,1:T(8,128)(2,1)S(1)}, u32[]{:S(2)}, u32[]{:S(2)}) collective-permute-start(bf16[256,512]{0,1:T(8,128)(2,1)S(1)} %fusion.37), channel_id=1, source_target_pairs={{0,7},{1,0},{2,1},{3,2},{4,3},{5,4},{6,5},{7,6},{8,15},{9,8},{10,9... | collective-permute-start | bytes 786440 | tf_op jit(solution)/shard_map/ppermute | solution.py:91
  233.2 9.8 %collective-permute-start.4 = (bf16[256,512]{0,1:T(8,128)(2,1)S(1)}, bf16[256,512]{0,1:T(8,128)(2,1)S(1)}, u32[]{:S(2)}, u32[]{:S(2)}) collective-permute-start(bf16[256,512]{0,1:T(8,128)(2,1)S(1)} %collective-permute-done.3), channel_id=1, source_target_pairs={{0,1},{1,2},{2,3},{3,4},{4,5},{5,6},{6,7},{7,0},{8,9},{9,10},{10,1... | collective-permute-start | bytes 786440 | tf_op jit(solution)/shard_map/ppermute | solution.py:89
  235.1 9.8 %collective-permute-start.7 = (bf16[256,512]{0,1:T(8,128)(2,1)S(1)}, bf16[256,512]{0,1:T(8,128)(2,1)S(1)}, u32[]{:S(2)}, u32[]{:S(2)}) collective-permute-start(bf16[256,512]{0,1:T(8,128)(2,1)S(1)} %collective-permute-done.6), channel_id=1, source_target_pairs={{0,7},{1,0},{2,1},{3,2},{4,3},{5,4},{6,5},{7,6},{8,15},{9,8},{10,9... | collective-permute-start | bytes 786440 | tf_op jit(solution)/shard_map/ppermute | solution.py:91
  243.0 9.5 %collective-permute-start.5 = (bf16[256,512]{0,1:T(8,128)(2,1)S(1)}, bf16[256,512]{0,1:T(8,128)(2,1)S(1)}, u32[]{:S(2)}, u32[]{:S(2)}) collective-permute-start(bf16[256,512]{0,1:T(8,128)(2,1)S(1)} %collective-permute-done.4), channel_id=1, source_target_pairs={{0,1},{1,2},{2,3},{3,4},{4,5},{5,6},{6,7},{7,0},{8,9},{9,10},{10,1... | collective-permute-start | bytes 786440 | tf_op jit(solution)/shard_map/ppermute | solution.py:89
  244.9 12.6 %collective-permute-start.8 = (bf16[256,512]{0,1:T(8,128)(2,1)S(1)}, bf16[256,512]{0,1:T(8,128)(2,1)S(1)}, u32[]{:S(2)}, u32[]{:S(2)}) collective-permute-start(bf16[256,512]{0,1:T(8,128)(2,1)S(1)} %collective-permute-done.7), channel_id=1, source_target_pairs={{0,7},{1,0},{2,1},{3,2},{4,3},{5,4},{6,5},{7,6},{8,15},{9,8},{10,9... | collective-permute-start | bytes 786440 | tf_op jit(solution)/shard_map/ppermute | solution.py:91
Sparse Core Ops, SparseCore 0:
  9.4 45.7 all-gather.3
  58.6 86.4 all-gather.5
  148.4 81.6 all-gather.7
